TPU v7x, 32 devices: a whole 2x2x4 slice. The times are simulated.
32 devices in a mesh: section: 2 (over y), dp: 4 (over x, core), tensor: 4 (over z).
Axes of the slice: x: 2, y: 2, z: 4, core: 2. Of those that a mesh axis runs over, the one named last changes fastest.
Arguments:
- master_weight: float32 [2304, 128, 128], P(('section', 'tensor'), 'dp'), parts along dimension 0, may hold values from -6 to 6
- first_moment: float32 [2304, 128, 128], P(('section', 'tensor'), 'dp'), parts along dimension 0, may hold values from -2 to 2
- second_moment: float32 [2304, 128, 128], P(('section', 'tensor'), 'dp'), parts along dimension 0, may hold values from 0.01 to 1
- grads: bfloat16 [4, 2304, 128, 128], P('dp', ('section', 'tensor')), parts along dimension 1, may hold values from -6 to 6
- dest_table: int32 [1152], replicated, may hold values from 0 to 1151, as said below
Outputs:
- weight_new: float32 [2304, 128, 128], P(('section', 'tensor'), 'dp'), parts along dimension 0
- first_new: float32 [2304, 128, 128], P(('section', 'tensor'), 'dp'), parts along dimension 0
- second_new: float32 [2304, 128, 128], P(('section', 'tensor'), 'dp'), parts along dimension 0
- weights: bfloat16 [2304, 128, 128], P(('section', 'tensor')), parts along dimension 0
There are 2 independent parts, one for each index of `section`. A program takes and returns all parts, laid end to end along the dimension named above; an argument that names none is the same for every part. Nothing has to cross between parts.
Inputs may be any that keep to these rules, and one draw needn't show every extreme that they name: `dest_table`: A permutation. Group old slots by s // 288 and new positions by p // 288: at most 72 slots of one group have positions in one block, and some pair of group and block has exactly 72.
All inputs are finite; a program needn't handle non-finite values.
Results may differ from a plain program's by a relative error of at most 0.0023.
Values may be sent and summed in bfloat16 or wider, within the bound.
A program may use at most 128 MiB of HBM per device.

v0:
```python
import functools
import math

import jax
import jax.numpy as jnp
from jax import lax
from jax.experimental import pallas as pl
from jax.experimental.pallas import tpu as pltpu
from jax.sharding import PartitionSpec as P

STEP = 10


learn_rate = 0.04
decay_rate = 1.5
beta_first = 0.9
beta_second = 0.95
epsilon = 1e-08


def adam_step(weight, first, second, grad):
    first_new = beta_first * first + (1.0 - beta_first) * grad
    second_new = beta_second * second + (1.0 - beta_second) * grad * grad
    first_hat = first_new * (1.0 / (1.0 - beta_first**STEP))
    second_hat = second_new * (1.0 / (1.0 - beta_second**STEP))
    weight_new = weight - learn_rate * (
        first_hat / (jnp.sqrt(second_hat) + epsilon) + decay_rate * weight
    )
    return (weight_new, first_new, second_new)


def routes(dest_table, slots, groups, capacity, rank_here):
    total = dest_table.shape[0]
    length = groups * capacity
    target = dest_table // slots
    local = dest_table % slots
    layout = target.reshape(groups, slots)
    order = jnp.arange(slots, dtype=jnp.int32)
    same = (layout[:, :, None] == layout[:, None, :]) & (order[None, :] < order[:, None])[None]
    within = jnp.sum(same.astype(jnp.int32), axis=2).reshape(total)
    source = jnp.arange(total, dtype=jnp.int32) // slots
    leaving = lax.dynamic_slice_in_dim(target * capacity + within, rank_here * slots, slots)
    places = jnp.arange(length, dtype=jnp.int32)
    outgoing = jnp.sum(jnp.where(leaving[None, :] == places[:, None], order[None, :], 0), axis=1)
    landing = jnp.where(target == rank_here, local, slots)
    incoming = jnp.sum(
        jnp.where(landing[None, :] == order[:, None], (source * capacity + within)[None, :], 0),
        axis=1,
    )
    return (outgoing, incoming)


ROWS = 8
SCALE = 8192.0
SPARE = 256 * 1024
PARTS = 4
MESH = pl.DeviceIdType.MESH


def encode(weight):
    scaled = weight * SCALE
    square = scaled * scaled
    fourth = square * square
    return (scaled * jnp.abs(scaled) * square * fourth).astype(jnp.bfloat16)


def decode(code):
    wide = code.astype(jnp.float32)
    root = jnp.sqrt(jnp.sqrt(jnp.sqrt(jnp.abs(wide)))) * (1.0 / SCALE)
    return jnp.where(wide < 0.0, -root, root)


def exchange_kernel(
    groups, replicas, capacity, chunks,
    outgoing, incoming, weight, first, second, grads,
    weight_new, first_new, second_new, weights,
    raw, sent, got, got_grads, rounded,
    load_sem, out_sem, own_sem, wide_send, wide_recv, grad_own, grad_send, grad_recv,
    last_own, last_send, last_recv, relay_send,
):
    slots, rows = weight.shape[0], weight.shape[1]
    parts = PARTS if slots % PARTS == 0 else 1
    me = lax.axis_index("tensor")
    mine = lax.axis_index("dp")
    hops = sorted(range(1, groups), key=lambda k: -min(k, groups - k))
    turns = range(1, replicas)

    def band(chunk, owner=None):
        start = chunk * ROWS if owner is None else owner * rows + chunk * ROWS
        return pl.ds(start, ROWS)

    def tiles(part):
        return pl.ds(part * (slots // parts), slots // parts)

    def loads(chunk):
        return [
            pltpu.make_async_copy(
                ref.at[:, band(chunk), :], raw[chunk % 2].at[k], load_sem.at[chunk % 2, k]
            )
            for k, ref in enumerate((weight, first, second))
        ]

    def wide(chunk, source, target):
        return pltpu.make_async_remote_copy(
            src_ref=sent.at[chunk, :, pl.ds(target * capacity, capacity)],
            dst_ref=got[chunk].at[:, pl.ds(source * capacity, capacity)],
            send_sem=wide_send.at[chunk, target],
            recv_sem=wide_recv.at[chunk, source],
            device_id={"tensor": target},
            device_id_type=MESH,
        )

    def own(chunk):
        here = pl.ds(me * capacity, capacity)
        return pltpu.make_async_copy(
            sent.at[chunk, :, here], got[chunk].at[:, here], own_sem.at[chunk]
        )

    def grad_copy(chunk, source, target):
        return pltpu.make_async_remote_copy(
            src_ref=grads.at[0, :, band(chunk, target), :],
            dst_ref=got_grads.at[source, chunk],
            send_sem=grad_send.at[chunk, target],
            recv_sem=grad_recv.at[chunk, source],
            device_id={"dp": target},
            device_id_type=MESH,
        )

    def grad_here(chunk):
        return pltpu.make_async_copy(
            grads.at[0, :, band(chunk, mine), :], got_grads.at[mine, chunk], grad_own.at[chunk]
        )

    def last_copy(chunk, part, source, target):
        return pltpu.make_async_remote_copy(
            src_ref=rounded.at[chunk, tiles(part)],
            dst_ref=weights.at[tiles(part), band(chunk, source), :],
            send_sem=last_send.at[chunk, part, target],
            recv_sem=last_recv.at[chunk, part, source],
            device_id={"dp": target},
            device_id_type=MESH,
        )

    def relay(chunk, part, source):
        rows_there = weights.at[tiles(part), band(chunk, source), :]
        return pltpu.make_async_remote_copy(
            src_ref=rows_there,
            dst_ref=rows_there,
            send_sem=relay_send.at[chunk, part, source],
            recv_sem=last_recv.at[chunk, part, source],
            device_id={"dp": twin},
            device_id_type=MESH,
        )

    def last_here(chunk):
        return pltpu.make_async_copy(
            rounded.at[chunk], weights.at[:, band(chunk, mine), :], last_own.at[chunk]
        )

    def stores(chunk):
        return [
            pltpu.make_async_copy(
                raw[chunk % 2].at[k], ref.at[:, band(chunk), :], out_sem.at[chunk % 2, k]
            )
            for k, ref in enumerate((weight_new, first_new, second_new))
        ]

    def start(copies):
        for copy in copies:
            copy.start()

    def finish(copies):
        for copy in copies:
            copy.wait()

    def partner(k):
        return lax.rem(me + k, groups)

    def peer(k):
        return lax.rem(mine + k, replicas)

    core = lax.rem(mine, 2)
    twin = mine + 1 - 2 * core
    across = range(1, replicas // 2)

    def far(k):
        return lax.rem(mine + 2 * k, replicas)

    def far_twin(k):
        return lax.rem(mine + 2 * k, replicas) + 1 - 2 * core

    start(loads(0))
    if chunks > 1:
        start(loads(1))
    barrier = pltpu.get_barrier_semaphore()
    for k in hops:
        pl.semaphore_signal(barrier, inc=1, device_id={"tensor": partner(k)}, device_id_type=MESH)
    for k in turns:
        pl.semaphore_signal(barrier, inc=1, device_id={"dp": peer(k)}, device_id_type=MESH)
    pl.semaphore_wait(barrier, groups - 1 + replicas - 1)

    for chunk in range(chunks):
        finish(loads(chunk))

        def pack(target, chunk=chunk):
            def one(i, carry):
                j = target * capacity + i
                s = outgoing[j]
                sent[chunk, 0, j] = encode(raw[chunk % 2][0, s])
                sent[chunk, 1, j] = raw[chunk % 2][1, s].astype(jnp.bfloat16)
                sent[chunk, 2, j] = raw[chunk % 2][2, s].astype(jnp.bfloat16)
                return carry

            lax.fori_loop(0, capacity, one, 0, unroll=math.gcd(capacity, 8))

        waiting = None
        for k in hops:
            pack(partner(k))
            if waiting is not None:
                waiting.start()
            waiting = wide(chunk, me, partner(k))
        pack(me)
        if waiting is not None:
            waiting.start()
        if chunk + 2 < chunks:
            start(loads(chunk + 2))
        own(chunk).start()
        start([grad_copy(chunk, mine, peer(k)) for k in turns])
        grad_here(chunk).start()

    for chunk in range(chunks):
        grad_here(chunk).wait()
        for k in turns:
            grad_copy(chunk, peer(k), mine).wait_recv()
        own(chunk).wait()
        for k in hops:
            wide(chunk, partner(k), me).wait_recv()
        if chunk >= 2:
            finish(stores(chunk - 2))

        def update(p, carry, chunk=chunk):
            j = incoming[p]
            grad = got_grads[0, chunk, p].astype(jnp.float32)
            for r in range(1, replicas):
                grad = grad + got_grads[r, chunk, p].astype(jnp.float32)
            weight_here, first_here, second_here = adam_step(
                decode(got[chunk][0, j]),
                got[chunk][1, j].astype(jnp.float32),
                got[chunk][2, j].astype(jnp.float32),
                grad * (1.0 / replicas),
            )
            rounded[chunk, p] = weight_here.astype(jnp.bfloat16)
            raw[chunk % 2][0, p] = weight_here
            raw[chunk % 2][1, p] = first_here
            raw[chunk % 2][2, p] = second_here
            return carry

        size = slots // parts
        for part in range(parts):
            lax.fori_loop(part * size, (part + 1) * size, update, 0, unroll=math.gcd(size, 8))
            start([last_copy(chunk, part, mine, far(k)) for k in across])
            last_copy(chunk, part, mine, twin).start()
        start(stores(chunk))
        last_here(chunk).start()

    pieces = [(chunk, part) for chunk in range(chunks) for part in range(parts)]
    for chunk, part in pieces:
        for k in across:
            last_copy(chunk, part, far(k), mine).wait_recv()
            relay(chunk, part, far(k)).start()

    for chunk, part in pieces:
        last_copy(chunk, part, twin, mine).wait_recv()
        last_copy(chunk, part, mine, twin).wait_send()
        for k in across:
            last_copy(chunk, part, mine, far(k)).wait_send()
            relay(chunk, part, far(k)).wait_send()
            relay(chunk, part, far_twin(k)).wait_recv()

    for chunk in range(chunks):
        last_here(chunk).wait()
        for k in turns:
            grad_copy(chunk, mine, peer(k)).wait_send()
        for k in hops:
            wide(chunk, me, partner(k)).wait_send()
        if chunk >= chunks - 2:
            finish(stores(chunk))


def exchange(outgoing, incoming, weight, first, second, grads, groups, replicas, capacity):
    slots, rows, lanes = weight.shape
    chunks = rows // ROWS
    length = groups * capacity
    whole = pltpu.VMEM(weight.shape, jnp.float32)
    anywhere = pl.BlockSpec(memory_space=pl.ANY)
    table = pl.BlockSpec(memory_space=pltpu.SMEM)
    dma = pltpu.SemaphoreType.DMA
    parts = PARTS if slots % PARTS == 0 else 1
    block = slots * ROWS * lanes
    scratch = block * (24 + 2 * chunks + 2 * chunks * replicas) + 12 * chunks * length * ROWS * lanes
    return pl.pallas_call(
        functools.partial(exchange_kernel, groups, replicas, capacity, chunks),
        out_shape=(whole, whole, whole, pltpu.VMEM(grads.shape[1:], jnp.bfloat16)),
        in_specs=[table, table] + [anywhere] * 4,
        out_specs=(anywhere,) * 4,
        scratch_shapes=[
            [pltpu.VMEM((3, slots, ROWS, lanes), jnp.float32)] * 2,
            pltpu.VMEM((chunks, 3, length, ROWS, lanes), jnp.bfloat16),
            [pltpu.VMEM((3, length, ROWS, lanes), jnp.bfloat16)] * chunks,
            pltpu.VMEM((replicas, chunks, slots, ROWS, lanes), jnp.bfloat16),
            pltpu.VMEM((chunks, slots, ROWS, lanes), jnp.bfloat16),
            dma((2, 3)),
            dma((2, 3)),
            dma((chunks,)),
            dma((chunks, groups)),
            dma((chunks, groups)),
            dma((chunks,)),
            dma((chunks, replicas)),
            dma((chunks, replicas)),
            dma((chunks,)),
            dma((chunks, parts, replicas)),
            dma((chunks, parts, replicas)),
            dma((chunks, parts, replicas)),
        ],
        compiler_params=pltpu.CompilerParams(
            collective_id=0, has_side_effects=True, vmem_limit_bytes=scratch + SPARE
        ),
        name="exchange",
    )(outgoing, incoming, weight, first, second, grads)


def shards(master_weight, first_moment, second_moment, grads, dest_table):
    groups = lax.axis_size("tensor")
    rank_here = lax.axis_index("tensor")
    slots = master_weight.shape[0]
    capacity = 2 * ((slots + 2 * groups - 1) // (2 * groups))
    outgoing, incoming = routes(dest_table, slots, groups, capacity, rank_here)
    replicas = lax.axis_size("dp")
    return exchange(
        outgoing, incoming, master_weight, first_moment, second_moment, grads,
        groups, replicas, capacity,
    )


def solution(mesh):
    placed = (
        P(("section", "tensor"), "dp", None),
        P(("section", "tensor"), "dp", None),
        P(("section", "tensor"), "dp", None),
        P("dp", ("section", "tensor"), None, None),
        P(),
    )
    return jax.shard_map(
        shards,
        mesh=mesh,
        in_specs=placed,
        out_specs=(
            P(("section", "tensor"), "dp", None),
            P(("section", "tensor"), "dp", None),
            P(("section", "tensor"), "dp", None),
            P(("section", "tensor"), None, None),
        ),
        check_vma=False,
    )
```

profile of v0, /device:TPU:9, one launch (start us, length us, event | category | flops | bytes accessed | tf_op | source)
XLA Modules:
  0.0 190.4 jit_solution(14148652689556404508)
XLA Ops:
  0.6 0.7 fusion.2
  1.3 0.1 eq.24
  1.5 0.6 convert_reduce_fusion
  2.1 0.1 reshape.46
  2.2 0.1 dynamic-slice_add_fusion
  2.3 0.8 select_reduce_fusion.incoming
  3.1 0.7 select_reduce_fusion.1.outgoing
  3.8 176.3 %exchange.1 = (f32[288,32,128]{2,1,0:T(8,128)S(1)}, f32[288,32,128]{2,1,0:T(8,128)S(1)}, f32[288,32,128]{2,1,0:T(8,128)S(1)}, bf16[288,128,128]{2,1,0:T(8,128)(2,1)S(1)}) custom-call(s32[288]{0:T(512)} %select_reduce_fusion.1.outgoing, s32[288]{0:T(512)} %select_reduce_fusion.incoming, f32[288,32,128]{2,1,0:T(8,128)} %weight.1, f32[288,32,128]{2,1,0:T(8,128)} %first.1, ...), custom_call_target="tpu_custom_call" | custom-call | tf_op jit(solution)/shard_map/exchange/pallas_call | solution.py:301
  180.1 2.2 %copy.13 = f32[288,32,128]{2,1,0:T(8,128)} copy(f32[288,32,128]{2,1,0:T(8,128)S(1)} %get-tuple-element.6) | data formatting | bytes 9437184
  182.3 2.2 %copy.14 = f32[288,32,128]{2,1,0:T(8,128)} copy(f32[288,32,128]{2,1,0:T(8,128)S(1)} %get-tuple-element.7) | data formatting | bytes 9437184
  184.5 2.2 %copy.15 = f32[288,32,128]{2,1,0:T(8,128)} copy(f32[288,32,128]{2,1,0:T(8,128)S(1)} %get-tuple-element.8) | data formatting | bytes 9437184
  186.7 3.7 %copy.16 = bf16[288,128,128]{2,1,0:T(8,128)(2,1)} copy(bf16[288,128,128]{2,1,0:T(8,128)(2,1)S(1)} %get-tuple-element.9) | data formatting | bytes 18874368
  (2 shorter events, 0.0 us)
where the time goes:
time: 191 us; the launch traced here: 190 us
  Pallas kernels  176 us (92%)
  local copies, waits for them, and re-layouts  10.5 us (5%)
  other arithmetic  3.03 us (2%)
    pallas_call x1, Pallas kernels, exchange(): pl.pallas_call(functools.partial(exchange_kernel, groups, replicas, capac...  176 us
    unnamed x4, local copies, waits for them, and re-layouts  10.3 us

commit v1 on v0

v1 whole, which is shorter than its diff:
```python
import functools
import math

import jax
import jax.numpy as jnp
from jax import lax
from jax.experimental import pallas as pl
from jax.experimental.pallas import tpu as pltpu
from jax.sharding import PartitionSpec as P

STEP = 10


learn_rate = 0.04
decay_rate = 1.5
beta_first = 0.9
beta_second = 0.95
epsilon = 1e-08


def adam_step(weight, first, second, grad):
    first_new = beta_first * first + (1.0 - beta_first) * grad
    second_new = beta_second * second + (1.0 - beta_second) * grad * grad
    first_hat = first_new * (1.0 / (1.0 - beta_first**STEP))
    second_hat = second_new * (1.0 / (1.0 - beta_second**STEP))
    weight_new = weight - learn_rate * (
        first_hat / (jnp.sqrt(second_hat) + epsilon) + decay_rate * weight
    )
    return (weight_new, first_new, second_new)


def routes(dest_table, slots, groups, capacity, rank_here):
    total = dest_table.shape[0]
    length = groups * capacity
    target = dest_table // slots
    local = dest_table % slots
    layout = target.reshape(groups, slots)
    order = jnp.arange(slots, dtype=jnp.int32)
    same = (layout[:, :, None] == layout[:, None, :]) & (order[None, :] < order[:, None])[None]
    within = jnp.sum(same.astype(jnp.int32), axis=2).reshape(total)
    source = jnp.arange(total, dtype=jnp.int32) // slots
    leaving = lax.dynamic_slice_in_dim(target * capacity + within, rank_here * slots, slots)
    places = jnp.arange(length, dtype=jnp.int32)
    outgoing = jnp.sum(jnp.where(leaving[None, :] == places[:, None], order[None, :], 0), axis=1)
    coming = jnp.where(target == rank_here, source * capacity + within, length)
    landing = jnp.sum(jnp.where(coming[None, :] == places[:, None], local[None, :] + 1, 0), axis=1)
    return (outgoing, landing - 1)


ROWS = 8
SCALE = 8192.0
SPARE = 256 * 1024
CUTS = 4
FEW = 8
MESH = pl.DeviceIdType.MESH


def encode(weight):
    scaled = weight * SCALE
    square = scaled * scaled
    fourth = square * square
    return (scaled * jnp.abs(scaled) * square * fourth).astype(jnp.bfloat16)


def decode(code):
    wide = code.astype(jnp.float32)
    root = jnp.sqrt(jnp.sqrt(jnp.sqrt(jnp.abs(wide)))) * (1.0 / SCALE)
    return jnp.where(wide < 0.0, -root, root)


def flipped(index, mask):
    for bit in range(mask.bit_length()):
        if mask >> bit & 1:
            index = index + (1 - 2 * lax.rem(index // 2**bit, 2)) * 2**bit
    return index


def loop(start, size, body):
    lax.fori_loop(0, size, lambda i, carry: (body(start + i), carry)[1], 0, unroll=math.gcd(size, 8))


def exchange_kernel(
    groups, replicas, capacity, chunks,
    outgoing, landing, weight, first, second, grads,
    weight_new, first_new, second_new, weights,
    raw, sent, got, own_here, own_far, twin_here, twin_far, far_here,
    load_sem, own_sem, wide_send, wide_recv, twin_send, twin_recv, far_send, far_recv,
    last_send, last_recv, relay_send,
):
    slots, rows = weight.shape[0], weight.shape[1]
    me = lax.axis_index("tensor")
    mine = lax.axis_index("dp")
    chips = replicas // 2
    core = lax.rem(mine, 2)
    twin = mine + 1 - 2 * core
    across = range(1, chips)
    power = groups & (groups - 1) == 0
    fine = groups <= FEW
    cuts = CUTS if fine and capacity % CUTS == 0 else 1
    hops = range(groups - 1, 0, -1)

    def partner(k):
        return flipped(me, k) if power else lax.rem(me + k, groups)

    def giver(k):
        return flipped(me, k) if power else lax.rem(me + groups - k, groups)

    def far(k):
        return lax.rem(mine + 2 * k, replicas)

    def far_twin(k):
        return lax.rem(mine + 2 * k, replicas) + 1 - 2 * core

    def band(chunk, owner=None):
        if owner is None:
            return pl.ds(chunk * ROWS, ROWS)
        return pl.ds(pl.multiple_of(owner * rows + chunk * ROWS, ROWS), ROWS)

    def pieces(chunk):
        return cuts if chunk == chunks - 1 else 1

    def loads(chunk):
        return [
            pltpu.make_async_copy(
                ref.at[:, band(chunk), :], raw[chunk % 2].at[k], load_sem.at[chunk % 2, k]
            )
            for k, ref in enumerate((weight, first, second))
        ]

    def wide(chunk, piece, k, source, target):
        size = capacity // pieces(chunk)
        return pltpu.make_async_remote_copy(
            src_ref=sent.at[chunk, :, pl.ds(target * capacity + piece * size, size)],
            dst_ref=got[chunk].at[:, pl.ds(source * capacity + piece * size, size)],
            send_sem=wide_send.at[chunk, piece, k],
            recv_sem=wide_recv.at[chunk, piece, k],
            device_id={"tensor": target},
            device_id_type=MESH,
        )

    def grad_loads(chunk):
        return [
            pltpu.make_async_copy(
                grads.at[0, :, band(chunk, far(k)), :], own_far.at[chunk, k - 1], own_sem.at[chunk, k]
            )
            if k
            else pltpu.make_async_copy(
                grads.at[0, :, band(chunk, mine), :], own_here[chunk], own_sem.at[chunk, 0]
            )
            for k in range(chips)
        ]

    def twin_copy(chunk, k):
        return pltpu.make_async_remote_copy(
            src_ref=grads.at[0, :, band(chunk, far_twin(k)), :],
            dst_ref=twin_far.at[chunk, k - 1] if k else twin_here[chunk],
            send_sem=twin_send.at[chunk, k],
            recv_sem=twin_recv.at[chunk, k],
            device_id={"dp": twin},
            device_id_type=MESH,
        )

    def far_copy(chunk, k):
        return pltpu.make_async_remote_copy(
            src_ref=own_far.at[chunk, k - 1],
            dst_ref=far_here[chunk][chips - k - 1],
            send_sem=far_send.at[chunk, k],
            recv_sem=far_recv.at[chunk, chips - k],
            device_id={"dp": far(k)},
            device_id_type=MESH,
        )

    def far_wait(chunk, k):
        return pltpu.make_async_remote_copy(
            src_ref=own_far.at[chunk, chips - k - 1],
            dst_ref=far_here[chunk][k - 1],
            send_sem=far_send.at[chunk, chips - k],
            recv_sem=far_recv.at[chunk, k],
            device_id={"dp": far(k)},
            device_id_type=MESH,
        )

    def steps(chunk):
        if not fine:
            return [([(0, k) for k in hops], 0, groups * capacity)]
        size = capacity // pieces(chunk)
        found = [([], me * capacity, capacity)]
        if pieces(chunk) > 1:
            found.append(([(i, 1) for i in range(pieces(chunk))], giver(1) * capacity, capacity))
            for i in range(pieces(chunk)):
                for k in range(groups - 1, 1, -1):
                    found.append(([(i, k)], giver(k) * capacity + i * size, size))
        else:
            for k in hops:
                found.append(([(0, k)], giver(k) * capacity, capacity))
        return found

    def spread(chunk, step, owner, target, send):
        _, start, size = steps(chunk)[step]
        here = weights.at[pl.ds(start, size), band(chunk, owner), :]
        return pltpu.make_async_remote_copy(
            src_ref=here,
            dst_ref=here,
            send_sem=send.at[chunk, step, lax.div(target, 2) if send is last_send else lax.div(owner, 2)],
            recv_sem=last_recv.at[chunk, step, owner],
            device_id={"dp": target},
            device_id_type=MESH,
        )

    def start(copies):
        for copy in copies:
            copy.start()

    def finish(copies):
        for copy in copies:
            copy.wait()

    start(loads(0))
    barrier = pltpu.get_barrier_semaphore()
    for k in hops:
        pl.semaphore_signal(barrier, inc=1, device_id={"tensor": partner(k)}, device_id_type=MESH)
    pl.semaphore_signal(barrier, inc=1, device_id={"dp": twin}, device_id_type=MESH)
    for k in across:
        pl.semaphore_signal(barrier, inc=1, device_id={"dp": far(k)}, device_id_type=MESH)
    for chunk in range(chunks):
        start(grad_loads(chunk))
    if chunks > 1:
        start(loads(1))

    def pack(chunk, target, source_of=None):
        def one(j):
            s = outgoing[j]
            place = j if source_of is None else source_of
            values = (
                encode(raw[chunk % 2][0, s]),
                raw[chunk % 2][1, s].astype(jnp.bfloat16),
                raw[chunk % 2][2, s].astype(jnp.bfloat16),
            )
            for k, value in enumerate(values):
                if source_of is None:
                    sent[chunk, k, j] = value
                else:
                    got[chunk][k, j] = value

        loop(target * capacity, capacity, one)

    waiting = []

    def send(copies):
        start(waiting)
        waiting[:] = copies

    for chunk in range(chunks):
        finish(loads(chunk))
        last = pieces(chunk) > 1
        for k in [1] * last + [k for k in hops if k > 1 or not last]:
            pack(chunk, partner(k))
            if chunk == 0 and k == groups - 1:
                pl.semaphore_wait(barrier, groups - 1 + chips)
                for other in range(chunks):
                    start([twin_copy(other, i) for i in reversed(range(chips))])
            if not last:
                send([wide(chunk, 0, k, me, partner(k))])
            elif k == 1:
                send([wide(chunk, i, 1, me, partner(1)) for i in range(cuts)])
        if last:
            send([
                wide(chunk, i, k, me, partner(k)) for i in range(cuts) for k in hops if k > 1
            ])
        pack(chunk, me, me)
        if chunk + 2 < chunks:
            start(loads(chunk + 2))
        send([])
        finish(grad_loads(chunk))
        for k in across:
            twin_copy(chunk, k).wait_recv()

            def join(s, chunk=chunk, k=k):
                total = own_far[chunk, k - 1, s].astype(jnp.float32) + twin_far[chunk, k - 1, s].astype(jnp.float32)
                own_far[chunk, k - 1, s] = total.astype(jnp.bfloat16)

            loop(0, slots, join)
            far_copy(chunk, k).start()

    def relay(chunk, step):
        for k in across:
            spread(chunk, step, far(k), twin, relay_send).wait_recv()
            spread(chunk, step, far(k), twin, relay_send).start()

    behind = []
    for chunk in range(chunks):
        twin_copy(chunk, 0).wait_recv()
        for k in across:
            far_wait(chunk, k).wait_recv()

        def update(j, chunk=chunk):
            p = jnp.maximum(landing[j], 0)
            grad = own_here[chunk][p].astype(jnp.float32) + twin_here[chunk][p].astype(jnp.float32)
            for k in across:
                grad = grad + far_here[chunk][k - 1][p].astype(jnp.float32)
            weight_here, first_here, second_here = adam_step(
                decode(got[chunk][0, j]),
                got[chunk][1, j].astype(jnp.float32),
                got[chunk][2, j].astype(jnp.float32),
                grad * (1.0 / replicas),
            )
            weights[j, band(chunk, mine)] = weight_here.astype(jnp.bfloat16)
            weight_new[j, band(chunk)] = weight_here
            first_new[j, band(chunk)] = first_here
            second_new[j, band(chunk)] = second_here

        for step, (waits, base, size) in enumerate(steps(chunk)):
            for piece, k in waits:
                wide(chunk, piece, k, giver(k), me).wait_recv()
            loop(base, size, update)
            start([spread(chunk, step, mine, far(k), last_send) for k in across])
            spread(chunk, step, mine, twin, last_send).start()
            behind.append((chunk, step))
            while len(behind) > 4:
                relay(*behind.pop(0))
    for chunk, step in behind:
        relay(chunk, step)

    for chunk in range(chunks):
        for step in range(len(steps(chunk))):
            spread(chunk, step, twin, twin, last_send).wait_recv()
            spread(chunk, step, mine, twin, last_send).wait_send()
            for k in across:
                spread(chunk, step, mine, far(k), last_send).wait_send()
                spread(chunk, step, far(k), twin, relay_send).wait_send()
                spread(chunk, step, far_twin(k), twin, relay_send).wait_recv()
    for chunk in range(chunks):
        for k in range(chips):
            twin_copy(chunk, k).wait_send()
        for k in across:
            far_copy(chunk, k).wait_send()
        for k in hops:
            for piece in range(pieces(chunk)):
                wide(chunk, piece, k, me, partner(k)).wait_send()


def place_kernel(landing, weight, first, second, weights, weight_new, first_new, second_new, weights_new, sem):
    length, slots = weight.shape[0], weight_new.shape[0]
    pairs = ((weight, weight_new), (first, first_new), (second, second_new), (weights, weights_new))

    def one(j, carry):
        p = landing[j]

        def move():
            for k, (source, target) in enumerate(pairs):
                pltpu.make_async_copy(source.at[j], target.at[p], sem.at[k]).start()

        if length == slots:
            move()
        else:
            pl.when(p >= 0)(move)
        return carry

    lax.fori_loop(0, length, one, 0, unroll=math.gcd(length, 8))
    for k, (source, target) in enumerate(pairs):
        pltpu.make_async_copy(source.at[pl.ds(0, slots)], target, sem.at[k]).wait()


def exchange(outgoing, landing, weight, first, second, grads, groups, replicas, capacity):
    slots, rows, lanes = weight.shape
    chunks = rows // ROWS
    chips = replicas // 2
    length = groups * capacity
    anywhere = pl.BlockSpec(memory_space=pl.ANY)
    near = pl.BlockSpec(memory_space=pltpu.VMEM)
    table = pl.BlockSpec(memory_space=pltpu.SMEM)
    dma = pltpu.SemaphoreType.DMA
    fine = groups <= FEW
    cuts = CUTS if fine and capacity % CUTS == 0 else 1
    most = 2 + (groups - 2) * cuts if fine else 1
    most = max(most, groups) if fine else 1
    half = jnp.bfloat16
    tile = ROWS * lanes
    scratch = (
        2 * 3 * slots * tile * 4
        + chunks * 2 * 3 * length * tile * 2
        + chunks * slots * tile * 2 * (2 + 3 * (chips - 1))
    )
    whole = pltpu.VMEM((length, rows, lanes), jnp.float32)
    results = pl.pallas_call(
        functools.partial(exchange_kernel, groups, replicas, capacity, chunks),
        out_shape=(whole, whole, whole, pltpu.VMEM((length,) + grads.shape[2:], half)),
        in_specs=[table, table] + [anywhere] * 4,
        out_specs=(near,) * 4,
        scratch_shapes=[
            [pltpu.VMEM((3, slots, ROWS, lanes), jnp.float32)] * 2,
            pltpu.VMEM((chunks, 3, length, ROWS, lanes), half),
            [pltpu.VMEM((3, length, ROWS, lanes), half)] * chunks,
            [pltpu.VMEM((slots, ROWS, lanes), half)] * chunks,
            pltpu.VMEM((chunks, chips - 1, slots, ROWS, lanes), half),
            [pltpu.VMEM((slots, ROWS, lanes), half)] * chunks,
            pltpu.VMEM((chunks, chips - 1, slots, ROWS, lanes), half),
            [[pltpu.VMEM((slots, ROWS, lanes), half)] * (chips - 1)] * chunks,
            dma((2, 3)),
            dma((chunks, chips)),
            dma((chunks, cuts, groups)),
            dma((chunks, cuts, groups)),
            dma((chunks, chips)),
            dma((chunks, chips)),
            dma((chunks, chips)),
            dma((chunks, chips)),
            dma((chunks, most, chips)),
            dma((chunks, most, replicas)),
            dma((chunks, most, chips)),
        ],
        compiler_params=pltpu.CompilerParams(
            collective_id=0, has_side_effects=True, vmem_limit_bytes=scratch + SPARE
        ),
        name="exchange",
    )(outgoing, landing, weight, first, second, grads)
    shape = jax.ShapeDtypeStruct(weight.shape, jnp.float32)
    return pl.pallas_call(
        place_kernel,
        out_shape=(shape, shape, shape, jax.ShapeDtypeStruct(grads.shape[1:], half)),
        in_specs=[table] + [anywhere] * 4,
        out_specs=(anywhere,) * 4,
        scratch_shapes=[dma((4,))],
        compiler_params=pltpu.CompilerParams(vmem_limit_bytes=SPARE),
        name="place",
    )(landing, *results)


def shards(master_weight, first_moment, second_moment, grads, dest_table):
    groups = lax.axis_size("tensor")
    rank_here = lax.axis_index("tensor")
    slots = master_weight.shape[0]
    capacity = 2 * ((slots + 2 * groups - 1) // (2 * groups))
    outgoing, landing = routes(dest_table, slots, groups, capacity, rank_here)
    replicas = lax.axis_size("dp")
    return exchange(
        outgoing, landing, master_weight, first_moment, second_moment, grads,
        groups, replicas, capacity,
    )


def solution(mesh):
    placed = (
        P(("section", "tensor"), "dp", None),
        P(("section", "tensor"), "dp", None),
        P(("section", "tensor"), "dp", None),
        P("dp", ("section", "tensor"), None, None),
        P(),
    )
    return jax.shard_map(
        shards,
        mesh=mesh,
        in_specs=placed,
        out_specs=(
            P(("section", "tensor"), "dp", None),
            P(("section", "tensor"), "dp", None),
            P(("section", "tensor"), "dp", None),
            P(("section", "tensor"), None, None),
        ),
        check_vma=False,
    )
```

time: 191 us -> 182 us (0.953); the launches traced: 190 us -> 179 us
  local copies, waits for them, and re-layouts: 10.5 us -> 0.16 us
  Pallas kernels: 176 us -> 174 us
    pallas_call x1, Pallas kernels: 176 us -> 166 us  [exchange(): pl.pallas_call(functools.partial(exchange_kernel, groups, replicas, capac...]
    unnamed x4 -> x2, local copies, waits for them, and re-layouts: 10.3 us -> 0.01 us
    pallas_call x0 -> x1, Pallas kernels: none -> 8.16 us  [exchange(): pl.pallas_call(place_kernel, out_shape=(shape, shape, shape, jax.ShapeDty...]
where the time goes in v1:
time: 182 us; the launch traced here: 179 us
  Pallas kernels  174 us (96%)
  other arithmetic  3.74 us (2%)
    pallas_call x1, Pallas kernels, exchange(): pl.pallas_call(functools.partial(exchange_kernel, groups, replicas, capac...  166 us
    pallas_call x1, Pallas kernels, exchange(): pl.pallas_call(place_kernel, out_shape=(shape, shape, shape, jax.ShapeDty...  8.16 us

profile of v1, /device:TPU:9, one launch (start us, length us, event | category | flops | bytes accessed | tf_op | source)
XLA Modules:
  0.0 178.6 jit_solution(16959888296235748345)
XLA Ops:
  0.6 0.7 add_select_fusion.2
  1.3 0.1 eq.49
  1.5 0.6 convert_reduce_fusion
  2.1 0.1 reshape.29
  2.2 0.1 dynamic-slice_add_fusion
  2.3 0.7 select_reduce_fusion.1.outgoing
  3.0 0.7 fusion.2
  3.7 0.2 select_reduce_fusion
  4.0 0.6 broadcast_add_fusion.landing
  4.5 0.0 copy-start
  4.6 165.8 %exchange.1 = (f32[288,32,128]{2,1,0:T(8,128)S(1)}, f32[288,32,128]{2,1,0:T(8,128)S(1)}, f32[288,32,128]{2,1,0:T(8,128)S(1)}, bf16[288,128,128]{2,1,0:T(8,128)(2,1)S(1)}) custom-call(s32[288]{0:T(512)} %select_reduce_fusion.1.outgoing, s32[288]{0:T(512)} %broadcast_add_fusion.landing, f32[288,32,128]{2,1,0:T(8,128)} %weight.1, f32[288,32,128]{2,1,0:T(8,128)} %first.1, ...), custom_call_target="tpu_custom_call" | custom-call | tf_op jit(solution)/shard_map/exchange/pallas_call | solution.py:385
  170.4 0.0 copy-done
  170.4 8.2 %place.1 = (f32[288,32,128]{2,1,0:T(8,128)}, f32[288,32,128]{2,1,0:T(8,128)}, f32[288,32,128]{2,1,0:T(8,128)}, bf16[288,128,128]{2,1,0:T(8,128)(2,1)}) custom-call(s32[288]{0:T(512)S(1)} %copy-done, f32[288,32,128]{2,1,0:T(8,128)S(1)} %get-tuple-element.8.weight, f32[288,32,128]{2,1,0:T(8,128)S(1)} %get-tuple-element.9.first, ...), custom_call_target="tpu_custom_call" | custom-call | tf_op jit(solution)/shard_map/place/pallas_call | solution.py:417
  (1 shorter events, 0.0 us)
Async XLA Ops:
  4.5 165.8 %copy-start = (s32[288]{0:T(512)S(1)}, s32[288]{0:T(512)}, u32[]{:S(2)}) copy-start(s32[288]{0:T(512)} %broadcast_add_fusion.landing) | copy-start | bytes 3460

commit v2 on v1

v2 whole, which is shorter than its diff:
```python
import functools
import math

import jax
import jax.numpy as jnp
from jax import lax
from jax.experimental import pallas as pl
from jax.experimental.pallas import tpu as pltpu
from jax.sharding import PartitionSpec as P

STEP = 10


learn_rate = 0.04
decay_rate = 1.5
beta_first = 0.9
beta_second = 0.95
epsilon = 1e-08


def adam_step(weight, first, second, grad):
    first_new = beta_first * first + (1.0 - beta_first) * grad
    second_new = beta_second * second + (1.0 - beta_second) * grad * grad
    first_hat = first_new * (1.0 / (1.0 - beta_first**STEP))
    second_hat = second_new * (1.0 / (1.0 - beta_second**STEP))
    weight_new = weight - learn_rate * (
        first_hat / (jnp.sqrt(second_hat) + epsilon) + decay_rate * weight
    )
    return (weight_new, first_new, second_new)


ROWS = 8
SCALE = 8192.0
SPARE = 512 * 1024
LANES = 128
HELD = 4096
LINE = 4
LAG = 4
MESH = pl.DeviceIdType.MESH


def encode(weight):
    scaled = weight * SCALE
    square = scaled * scaled
    fourth = square * square
    return (scaled * jnp.abs(scaled) * square * fourth).astype(jnp.bfloat16)


def decode(code):
    wide = code.astype(jnp.float32)
    root = jnp.sqrt(jnp.sqrt(jnp.sqrt(jnp.abs(wide)))) * (1.0 / SCALE)
    return jnp.where(wide < 0.0, -root, root)


def loop(start, size, body):
    lax.fori_loop(0, size, lambda i, carry: (body(start + i), carry)[1], 0, unroll=math.gcd(size, 8))


def rows_from(flat, groups, slots):
    width = LANES * pl.cdiv(slots, LANES)
    found = []
    for group in range(groups):
        first, extra = divmod(group * slots, LANES)
        count = pl.cdiv(extra + slots, LANES)
        row = [flat[first + i : first + i + 1] for i in range(count)]
        row = jnp.concatenate(row, axis=1) if count > 1 else row[0]
        if extra:
            row = pltpu.roll(row, count * LANES - extra, 1)
        found.append(row[:, :width])
    spare = -groups % 8
    if spare:
        found.append(jnp.zeros((spare, width), jnp.int32))
    return jnp.concatenate(found, axis=0)


def routes(flat, groups, slots, me):
    dest = rows_from(flat, groups, slots)
    width = dest.shape[1]
    lane = lax.broadcasted_iota(jnp.int32, dest.shape, 1)
    line = lax.broadcasted_iota(jnp.int32, dest.shape, 0)
    target = jnp.where((lane < slots) & (line < groups), 0, -groups)
    for group in range(1, groups):
        target = target + (dest >= group * slots).astype(jnp.int32)
    leaving = jnp.sum(jnp.where(line == me, target, 0), axis=0, keepdims=True)
    coming = jnp.where(target == me, 1, 0)
    going = jnp.where(leaving == line, 1, 0)
    table = jnp.concatenate([coming, going], axis=0)
    value = jnp.concatenate([dest - me * slots, lane], axis=0)
    lane = jnp.concatenate([lane, lane], axis=0)
    before = table
    step = 1
    while step < slots:
        before = before + jnp.where(lane >= step, pltpu.roll(before, step, 1), 0)
        step *= 2
    held = jnp.where(table > 0, value + 1 + HELD * (lane + 1 - before), 0)
    step = 1
    while step < slots:
        moved = jnp.where(jnp.bitwise_and(held, HELD * step) > 0, held, 0)
        held = held - moved + pltpu.roll(moved, width - step, 1)
        step *= 2
    return jnp.bitwise_and(held, HELD - 1) - 1


def cut_of(groups, capacity):
    if groups == LINE and capacity % 8 == 0 and capacity > 32:
        return (capacity - 32, 16, 8, 8)
    return (capacity,)


def schedule(groups, chunks, cuts):
    if groups != LINE:
        return [(chunk, None, 0) for chunk in range(chunks)]
    last = chunks - 1
    timed = []
    for chunk in range(chunks):
        timed.append((chunk + 1.6, chunk, 0, 0))
        timed.append((chunk + 2.0, chunk, 1, 0))
        for role, when in ((2, 2.3), (3, 3.7)):
            count = cuts if chunk == last else 1
            late = last + 10.0 * role if chunk == last else chunk * 2.0 + when
            timed += [(late + piece, chunk, role, piece) for piece in range(count)]
    return [entry[1:] for entry in sorted(timed)]


def exchange_kernel(
    groups, replicas, capacity, chunks,
    dest, weight, first, second, grads,
    weight_new, first_new, second_new, weights, table_out,
    table, flat,
    raw, sent, got, own_here, own_far, twin_here, twin_far, far_here,
    table_sem, load_sem, own_sem, wide_send, wide_recv, twin_send, twin_recv, far_send, far_recv,
    last_send, last_recv, twin_last, relay_send, relay_recv,
):
    slots, rows = weight.shape[0], weight.shape[1]
    me = lax.axis_index("tensor")
    mine = lax.axis_index("dp")
    chips = replicas // 2
    core = lax.rem(mine, 2)
    twin = mine + 1 - 2 * core
    across = range(1, chips)
    line = groups == LINE
    cuts = cut_of(groups, capacity)
    order = schedule(groups, chunks, len(cuts))
    if line:
        side = me // 2
        near = me + 1 - 2 * lax.rem(me, 2)
        targets = [3 - me, lax.rem(me + 2, 4), near]
        sources = [me, near, 3 - 3 * side, 2 - side]
    else:
        targets = [lax.rem(me + k, groups) for k in range(1, groups)]
        sources = [lax.rem(me + groups - k, groups) for k in range(groups)]

    def far(k):
        return lax.rem(mine + 2 * k, replicas)

    def far_twin(k):
        return lax.rem(mine + 2 * k, replicas) + 1 - 2 * core

    def band(chunk, owner=None):
        if owner is None:
            return pl.ds(chunk * ROWS, ROWS)
        return pl.ds(pl.multiple_of(owner * rows + chunk * ROWS, ROWS), ROWS)

    def loads(chunk):
        return [
            pltpu.make_async_copy(
                ref.at[:, band(chunk), :], raw[chunk % 2].at[k], load_sem.at[chunk % 2]
            )
            for k, ref in enumerate((weight, first, second))
        ]

    def loaded(chunk):
        return pltpu.make_async_copy(raw[chunk % 2], raw[chunk % 2], load_sem.at[chunk % 2])

    def cut(chunk, piece, split):
        if chunk == chunks - 1 and split:
            return sum(cuts[:piece]), cuts[piece]
        return 0, capacity

    def wide(chunk, piece, split, source, target):
        begin, size = cut(chunk, piece, split)
        return pltpu.make_async_remote_copy(
            src_ref=sent.at[chunk, :, pl.ds(target * capacity + begin, size)],
            dst_ref=got[chunk].at[:, pl.ds(source * capacity + begin, size)],
            send_sem=wide_send.at[chunk],
            recv_sem=wide_recv.at[chunk + piece, source],
            device_id={"tensor": target},
            device_id_type=MESH,
        )

    def wide_sent(chunk):
        everything = sent.at[chunk, :, pl.ds(0, (groups - 1) * capacity)]
        return pltpu.make_async_remote_copy(
            src_ref=everything,
            dst_ref=everything,
            send_sem=wide_send.at[chunk],
            recv_sem=wide_recv.at[chunk, 0],
            device_id={"tensor": targets[0]},
            device_id_type=MESH,
        )

    def grad_loads(chunk):
        return [
            pltpu.make_async_copy(
                grads.at[0, :, band(chunk, far(k)), :], own_far.at[chunk, k - 1], own_sem.at[chunk, k]
            )
            if k
            else pltpu.make_async_copy(
                grads.at[0, :, band(chunk, mine), :], own_here[chunk], own_sem.at[chunk, 0]
            )
            for k in range(chips)
        ]

    def twin_copy(chunk, k):
        return pltpu.make_async_remote_copy(
            src_ref=grads.at[0, :, band(chunk, far_twin(k)), :],
            dst_ref=twin_far.at[chunk, k - 1] if k else twin_here[chunk],
            send_sem=twin_send.at[k],
            recv_sem=twin_recv.at[chunk, k],
            device_id={"dp": twin},
            device_id_type=MESH,
        )

    def far_copy(chunk, k):
        return pltpu.make_async_remote_copy(
            src_ref=own_far.at[chunk, k - 1],
            dst_ref=far_here[chunk][chips - k - 1],
            send_sem=far_send.at[k],
            recv_sem=far_recv.at[chunk, chips - k],
            device_id={"dp": far(k)},
            device_id_type=MESH,
        )

    def far_wait(chunk, k):
        return pltpu.make_async_remote_copy(
            src_ref=own_far.at[chunk, chips - k - 1],
            dst_ref=far_here[chunk][k - 1],
            send_sem=far_send.at[chips - k],
            recv_sem=far_recv.at[chunk, k],
            device_id={"dp": far(k)},
            device_id_type=MESH,
        )

    def extent(entry):
        chunk, role, piece = entry
        if role is None:
            return 0, groups * capacity
        begin, size = cut(chunk, piece, role > 1)
        return sources[role] * capacity + begin, size

    def rows_of(entry):
        if entry[1] is None:
            return [(source, 0, capacity) for source in range(groups)]
        return [(sources[entry[1]], *cut(entry[0], entry[2], entry[1] > 1))]

    def spread(step, owner, target, send, recv):
        start, size = extent(order[step])
        here = weights.at[pl.ds(start, size), band(order[step][0], owner), :]
        return pltpu.make_async_remote_copy(
            src_ref=here,
            dst_ref=here,
            send_sem=send,
            recv_sem=recv,
            device_id={"dp": target},
            device_id_type=MESH,
        )

    def far_spread(step, k):
        return spread(step, mine, far(k), last_send.at[k], last_recv.at[step, chips - k - 1])

    def twin_spread(step):
        return spread(step, mine, twin, last_send.at[0], twin_last.at[0])

    def relay(step, k):
        return spread(step, far(k), twin, relay_send.at[k], relay_recv.at[k])

    def whole(owner, send, recv):
        here = weights.at[:, pl.ds(pl.multiple_of(owner * rows, ROWS), rows), :]
        return pltpu.make_async_remote_copy(
            src_ref=here,
            dst_ref=here,
            send_sem=send,
            recv_sem=recv,
            device_id={"dp": twin},
            device_id_type=MESH,
        )

    def every(ref, send, recv):
        return pltpu.make_async_remote_copy(
            src_ref=ref, dst_ref=ref, send_sem=send, recv_sem=recv,
            device_id={"dp": twin}, device_id_type=MESH,
        )

    def start(copies):
        for copy in copies:
            copy.start()

    fetch = pltpu.make_async_copy(dest, flat, table_sem.at[0])
    fetch.start()
    start(loads(0))
    barrier = pltpu.get_barrier_semaphore()
    for target in targets:
        pl.semaphore_signal(barrier, inc=1, device_id={"tensor": target}, device_id_type=MESH)
    pl.semaphore_signal(barrier, inc=1, device_id={"dp": twin}, device_id_type=MESH)
    for k in across:
        pl.semaphore_signal(barrier, inc=1, device_id={"dp": far(k)}, device_id_type=MESH)
    half = table_out.shape[0] // 2
    fetch.wait()
    table_out[...] = routes(flat[...], groups, slots, me)[:, : table_out.shape[1]]
    start(grad_loads(0))
    copy = pltpu.make_async_copy(table_out, table, table_sem.at[1])
    copy.start()
    copy.wait()

    def pack(chunk, target, to_got=False):
        def one(i):
            s = jnp.maximum(table[half + target, i], 0)
            j = target * capacity + i
            values = (
                encode(raw[chunk % 2][0, s]),
                raw[chunk % 2][1, s].astype(jnp.bfloat16),
                raw[chunk % 2][2, s].astype(jnp.bfloat16),
            )
            for k, value in enumerate(values):
                if to_got:
                    got[chunk][k, j] = value
                else:
                    sent[chunk, k, j] = value

        loop(0, capacity, one)

    waiting = []

    def send(copies):
        start(waiting)
        waiting[:] = copies

    for chunk in range(chunks):
        loaded(chunk).wait()
        if chunk == 0:
            for other in range(1, chunks):
                start(grad_loads(other))
            if chunks > 1:
                start(loads(1))
        split = chunk == chunks - 1 and len(cuts) > 1
        for i, target in enumerate(targets):
            pack(chunk, target)
            if chunk == 0 and i == 0:
                pl.semaphore_wait(barrier, groups - 1 + chips)
                for other in range(chunks):
                    start([twin_copy(other, k) for k in reversed(range(chips))])
            if not split:
                send([wide(chunk, 0, False, me, target)])
        if split:
            send(
                [wide(chunk, 0, False, me, targets[-1])]
                + [
                    wide(chunk, i, True, me, target)
                    for i in range(len(cuts))
                    for target in targets[:-1]
                ]
            )
        pack(chunk, me, True)
        if chunk + 2 < chunks:
            start(loads(chunk + 2))
        send([])
        for copy in grad_loads(chunk):
            copy.wait()
        for k in across:
            twin_copy(chunk, k).wait_recv()

            def join(s, chunk=chunk, k=k):
                total = own_far[chunk, k - 1, s].astype(jnp.float32) + twin_far[
                    chunk, k - 1, s
                ].astype(jnp.float32)
                own_far[chunk, k - 1, s] = total.astype(jnp.bfloat16)

            loop(0, slots, join)
            far_copy(chunk, k).start()

    def pass_on(step):
        for k in across:
            far_wait_here = spread(step, far(k), twin, relay_send.at[k], last_recv.at[step, k - 1])
            far_wait_here.wait_recv()
            relay(step, k).start()

    ready = set()
    for step, entry in enumerate(order):
        chunk, role, piece = entry
        if chunk not in ready:
            ready.add(chunk)
            twin_copy(chunk, 0).wait_recv()
            for k in across:
                far_wait(chunk, k).wait_recv()
        if role is None:
            for source in sources[1:]:
                wide(chunk, 0, False, source, me).wait_recv()
        elif role > 0:
            wide(chunk, piece, role > 1, sources[role], me).wait_recv()

        def update(source, i, chunk=chunk):
            p = jnp.maximum(table[source, i], 0)
            j = source * capacity + i
            grad = own_here[chunk][p].astype(jnp.float32) + twin_here[chunk][p].astype(jnp.float32)
            for k in across:
                grad = grad + far_here[chunk][k - 1][p].astype(jnp.float32)
            weight_here, first_here, second_here = adam_step(
                decode(got[chunk][0, j]),
                got[chunk][1, j].astype(jnp.float32),
                got[chunk][2, j].astype(jnp.float32),
                grad * (1.0 / replicas),
            )
            weights[j, band(chunk, mine)] = weight_here.astype(jnp.bfloat16)
            weight_new[j, band(chunk)] = weight_here
            first_new[j, band(chunk)] = first_here
            second_new[j, band(chunk)] = second_here

        for source, begin, size in rows_of(entry):
            loop(begin, size, functools.partial(update, source))
        start([far_spread(step, k) for k in across])
        twin_spread(step).start()
        if step >= LAG:
            pass_on(step - LAG)
    for step in range(max(len(order) - LAG, 0), len(order)):
        pass_on(step)

    whole(twin, last_send.at[0], twin_last.at[0]).wait_recv()
    whole(mine, last_send.at[0], twin_last.at[0]).wait_send()
    for k in across:
        whole(mine, last_send.at[k], twin_last.at[0]).wait_send()
        whole(far(k), relay_send.at[k], relay_recv.at[k]).wait_send()
        whole(far_twin(k), relay_send.at[k], relay_recv.at[k]).wait_recv()
        every(own_far.at[:, k - 1], far_send.at[k], far_recv.at[0, 0]).wait_send()
    for k in range(chips):
        every(twin_far.at[:, max(k - 1, 0)], twin_send.at[k], twin_recv.at[0, 0]).wait_send()
    for chunk in range(chunks):
        wide_sent(chunk).wait_send()


def place_kernel(
    groups, capacity, table, weight, first, second, weights,
    weight_new, first_new, second_new, weights_new, sem,
):
    slots = weight_new.shape[0]
    pairs = ((weight, weight_new), (first, first_new), (second, second_new), (weights, weights_new))

    def one(source, i):
        p = table[source, i]
        j = source * capacity + i

        def move():
            for k, (held, target) in enumerate(pairs):
                pltpu.make_async_copy(held.at[j], target.at[p], sem.at[k]).start()

        if groups * capacity == slots:
            move()
        else:
            pl.when(p >= 0)(move)

    for source in range(groups):
        loop(0, capacity, functools.partial(one, source))
    for k, (held, target) in enumerate(pairs):
        pltpu.make_async_copy(held.at[pl.ds(0, slots)], target, sem.at[k]).wait()


def exchange(dest_table, weight, first, second, grads, groups, replicas, capacity):
    slots, rows, lanes = weight.shape
    chunks = rows // ROWS
    chips = replicas // 2
    length = groups * capacity
    lines = 8 * pl.cdiv(groups, 8)
    wide = LANES * pl.cdiv(capacity, LANES)
    spare = -dest_table.shape[0] % LANES
    dest = jnp.pad(dest_table, (0, spare)) if spare else dest_table
    dest = dest.reshape(-1, LANES)
    anywhere = pl.BlockSpec(memory_space=pl.ANY)
    near = pl.BlockSpec(memory_space=pltpu.VMEM)
    table = pl.BlockSpec(memory_space=pltpu.SMEM)
    dma = pltpu.SemaphoreType.DMA
    cuts = len(cut_of(groups, capacity))
    steps = len(schedule(groups, chunks, cuts))
    half = jnp.bfloat16
    tile = ROWS * lanes
    scratch = (
        2 * 3 * slots * tile * 4
        + chunks * 2 * 3 * length * tile * 2
        + chunks * slots * tile * 2 * (2 + 3 * (chips - 1))
    )
    whole = pltpu.VMEM((length, rows, lanes), jnp.float32)
    *results, routed = pl.pallas_call(
        functools.partial(exchange_kernel, groups, replicas, capacity, chunks),
        out_shape=(
            whole, whole, whole,
            pltpu.VMEM((length,) + grads.shape[2:], half),
            pltpu.VMEM((2 * lines, wide), jnp.int32),
        ),
        in_specs=[anywhere] * 5,
        out_specs=(near,) * 5,
        scratch_shapes=[
            pltpu.SMEM((2 * lines, wide), jnp.int32),
            pltpu.VMEM(dest.shape, jnp.int32),
            [pltpu.VMEM((3, slots, ROWS, lanes), jnp.float32)] * 2,
            pltpu.VMEM((chunks, 3, length, ROWS, lanes), half),
            [pltpu.VMEM((3, length, ROWS, lanes), half)] * chunks,
            [pltpu.VMEM((slots, ROWS, lanes), half)] * chunks,
            pltpu.VMEM((chunks, chips - 1, slots, ROWS, lanes), half),
            [pltpu.VMEM((slots, ROWS, lanes), half)] * chunks,
            pltpu.VMEM((chunks, chips - 1, slots, ROWS, lanes), half),
            [[pltpu.VMEM((slots, ROWS, lanes), half)] * (chips - 1)] * chunks,
            dma((2,)),
            dma((2,)),
            dma((chunks, chips)),
            dma((chunks,)),
            dma((chunks + cuts - 1, groups)),
            dma((chips,)),
            dma((chunks, chips)),
            dma((chips,)),
            dma((chunks, chips)),
            dma((chips,)),
            dma((steps, chips - 1)),
            dma((1,)),
            dma((chips,)),
            dma((chips,)),
        ],
        compiler_params=pltpu.CompilerParams(
            collective_id=0, has_side_effects=True, vmem_limit_bytes=scratch + SPARE
        ),
        name="exchange",
    )(dest, weight, first, second, grads)
    shape = jax.ShapeDtypeStruct(weight.shape, jnp.float32)
    return pl.pallas_call(
        functools.partial(place_kernel, groups, capacity),
        out_shape=(shape, shape, shape, jax.ShapeDtypeStruct(grads.shape[1:], half)),
        in_specs=[table] + [anywhere] * 4,
        out_specs=(anywhere,) * 4,
        scratch_shapes=[dma((4,))],
        compiler_params=pltpu.CompilerParams(vmem_limit_bytes=SPARE),
        name="place",
    )(routed, *results)


def shards(master_weight, first_moment, second_moment, grads, dest_table):
    groups = lax.axis_size("tensor")
    slots = master_weight.shape[0]
    capacity = 2 * ((slots + 2 * groups - 1) // (2 * groups))
    replicas = lax.axis_size("dp")
    return exchange(
        dest_table, master_weight, first_moment, second_moment, grads,
        groups, replicas, capacity,
    )


def solution(mesh):
    placed = (
        P(("section", "tensor"), "dp", None),
        P(("section", "tensor"), "dp", None),
        P(("section", "tensor"), "dp", None),
        P("dp", ("section", "tensor"), None, None),
        P(),
    )
    return jax.shard_map(
        shards,
        mesh=mesh,
        in_specs=placed,
        out_specs=(
            P(("section", "tensor"), "dp", None),
            P(("section", "tensor"), "dp", None),
            P(("section", "tensor"), "dp", None),
            P(("section", "tensor"), None, None),
        ),
        check_vma=False,
    )
```

time: 182 us -> 174 us (0.956)
  other arithmetic: 3.74 us -> 0 us
  Pallas kernels: 174 us -> 171 us
    pallas_call x1, Pallas kernels: 166 us -> 163 us  [exchange(): pl.pallas_call(functools.partial(exchange_kernel, groups, replicas, capac...]
where the time goes in v2:
time: 174 us; the launch traced here: 172 us
  Pallas kernels  171 us (98%)
    pallas_call x1, Pallas kernels, exchange(): pl.pallas_call(functools.partial(exchange_kernel, groups, replicas, capac...  163 us
    pallas_call x1, Pallas kernels, exchange(): pl.pallas_call(functools.partial(place_kernel, groups, capacity), out_sha...  8.27 us

profile of v2, /device:TPU:9, one launch (start us, length us, event | category | flops | bytes accessed | tf_op | source)
XLA Modules:
  0.0 171.8 jit_solution(7493240975388295129)
XLA Ops:
  0.6 162.9 %exchange.1 = (f32[288,32,128]{2,1,0:T(8,128)S(1)}, f32[288,32,128]{2,1,0:T(8,128)S(1)}, f32[288,32,128]{2,1,0:T(8,128)S(1)}, bf16[288,128,128]{2,1,0:T(8,128)(2,1)S(1)}, s32[16,128]{1,0:T(8,128)S(1)}) custom-call(s32[9,128]{1,0:T(8,128)} %bitcast.1, f32[288,32,128]{2,1,0:T(8,128)} %weight.1, f32[288,32,128]{2,1,0:T(8,128)} %first.1, ...), custom_call_target="tpu_custom_call" | custom-call | tf_op jit(solution)/shard_map/exchange/pallas_call | solution.py:490
  163.5 8.3 %place.1 = (f32[288,32,128]{2,1,0:T(8,128)}, f32[288,32,128]{2,1,0:T(8,128)}, f32[288,32,128]{2,1,0:T(8,128)}, bf16[288,128,128]{2,1,0:T(8,128)(2,1)}) custom-call(s32[16,128]{1,0:T(8,128)S(1)} %get-tuple-element.9.table, f32[288,32,128]{2,1,0:T(8,128)S(1)} %get-tuple-element.10.weight, f32[288,32,128]{2,1,0:T(8,128)S(1)} %get-tuple-element.11.first, ...), custom_call_target="tpu_custom_call" | custom-call | tf_op jit(solution)/shard_map/place/pallas_call | solution.py:531

commit v3 on v2

--- a/solution.py
+++ b/solution.py
@@ -36,6 +36,7 @@
 HELD = 4096
 LINE = 4
 LAG = 4
+DIRECT = 2
 MESH = pl.DeviceIdType.MESH
 
 
@@ -67,37 +68,47 @@
         if extra:
             row = pltpu.roll(row, count * LANES - extra, 1)
         found.append(row[:, :width])
-    spare = -groups % 8
-    if spare:
-        found.append(jnp.zeros((spare, width), jnp.int32))
-    return jnp.concatenate(found, axis=0)
-
-
-def routes(flat, groups, slots, me):
-    dest = rows_from(flat, groups, slots)
-    width = dest.shape[1]
-    lane = lax.broadcasted_iota(jnp.int32, dest.shape, 1)
-    line = lax.broadcasted_iota(jnp.int32, dest.shape, 0)
-    target = jnp.where((lane < slots) & (line < groups), 0, -groups)
+    return found
+
+
+def lines_of(groups):
+    return groups if groups % 4 == 0 else 8 * pl.cdiv(groups, 8)
+
+
+def routes(flat, groups, slots, capacity, me):
+    rows = rows_from(flat, groups, slots)
+    width = rows[0].shape[1]
+    lines = lines_of(groups)
+    leaving = rows[0]
     for group in range(1, groups):
-        target = target + (dest >= group * slots).astype(jnp.int32)
-    leaving = jnp.sum(jnp.where(line == me, target, 0), axis=0, keepdims=True)
-    coming = jnp.where(target == me, 1, 0)
-    going = jnp.where(leaving == line, 1, 0)
-    table = jnp.concatenate([coming, going], axis=0)
-    value = jnp.concatenate([dest - me * slots, lane], axis=0)
-    lane = jnp.concatenate([lane, lane], axis=0)
-    before = table
+        leaving = jnp.where(me == group, rows[group], leaving)
+    unused = [jnp.full_like(leaving, -1)] * (lines - groups)
+    table = jnp.concatenate(rows + unused + [leaving] * groups + unused, axis=0)
+    lane = lax.broadcasted_iota(jnp.int32, table.shape, 1)
+    line = lax.broadcasted_iota(jnp.int32, table.shape, 0)
+    table = table - jnp.where(line < lines, me, line - lines) * slots
+    taken = (table >= 0) & (table < slots) & (lane < slots)
+    taken = taken & (jnp.where(line < lines, line, line - lines) < groups)
+    before = taken.astype(jnp.int32)
     step = 1
     while step < slots:
-        before = before + jnp.where(lane >= step, pltpu.roll(before, step, 1), 0)
-        step *= 2
-    held = jnp.where(table > 0, value + 1 + HELD * (lane + 1 - before), 0)
+        total = before
+        for shift in range(step, min(4 * step, slots), step):
+            total = total + jnp.where(lane >= shift, pltpu.roll(before, shift, 1), 0)
+        before = total
+        step *= 4
+    held = jnp.where(line < lines, table, lane) + 1 + HELD * (lane + 1 - before)
+    held = jnp.where(taken, held, 0)
+    reach = slots - capacity if groups * capacity == slots else slots - 1
     step = 1
-    while step < slots:
-        moved = jnp.where(jnp.bitwise_and(held, HELD * step) > 0, held, 0)
-        held = held - moved + pltpu.roll(moved, width - step, 1)
-        step *= 2
+    while step <= reach:
+        digit = jnp.bitwise_and(held, 3 * HELD * step)
+        total = jnp.where(digit == 0, held, 0)
+        for shift in range(step, min(4 * step, reach + 1), step):
+            moved = jnp.where(digit == HELD * shift, held, 0)
+            total = total + pltpu.roll(moved, width - shift, 1)
+        held = total
+        step *= 4
     return jnp.bitwise_and(held, HELD - 1) - 1
 
 
@@ -116,7 +127,7 @@
         timed.append((chunk + 1.6, chunk, 0, 0))
         timed.append((chunk + 2.0, chunk, 1, 0))
         for role, when in ((2, 2.3), (3, 3.7)):
-            count = cuts if chunk == last else 1
+            count = cuts if chunk == last and role == 3 else 1
             late = last + 10.0 * role if chunk == last else chunk * 2.0 + when
             timed += [(late + piece, chunk, role, piece) for piece in range(count)]
     return [entry[1:] for entry in sorted(timed)]
@@ -129,7 +140,7 @@
     table, flat,
     raw, sent, got, own_here, own_far, twin_here, twin_far, far_here,
     table_sem, load_sem, own_sem, wide_send, wide_recv, twin_send, twin_recv, far_send, far_recv,
-    last_send, last_recv, twin_last, relay_send, relay_recv,
+    last_send, last_recv, twin_last, relay_send, relay_recv, direct_send,
 ):
     slots, rows = weight.shape[0], weight.shape[1]
     me = lax.axis_index("tensor")
@@ -141,6 +152,9 @@
     line = groups == LINE
     cuts = cut_of(groups, capacity)
     order = schedule(groups, chunks, len(cuts))
+    straight = sum(cuts[-DIRECT:]) if line and len(cuts) > DIRECT else 0
+    straight = 0 if straight * ROWS % rows else straight
+    relayed = len(order) - (DIRECT if straight else 0)
     if line:
         side = me // 2
         near = me + 1 - 2 * lax.rem(me, 2)
@@ -164,59 +178,65 @@
     def loads(chunk):
         return [
             pltpu.make_async_copy(
-                ref.at[:, band(chunk), :], raw[chunk % 2].at[k], load_sem.at[chunk % 2]
+                ref.at[:, band(chunk), :],
+                raw[chunk % 2][k],
+                load_sem.at[chunk % 2, k],
             )
             for k, ref in enumerate((weight, first, second))
         ]
-
-    def loaded(chunk):
-        return pltpu.make_async_copy(raw[chunk % 2], raw[chunk % 2], load_sem.at[chunk % 2])
 
     def cut(chunk, piece, split):
         if chunk == chunks - 1 and split:
             return sum(cuts[:piece]), cuts[piece]
         return 0, capacity
 
-    def wide(chunk, piece, split, source, target):
+    def slot(chunk, role, piece):
+        last = chunks - 1
+        return 3 * chunk + role - 1 + (piece if role == 3 and chunk == last else 0)
+
+    def slot_there(chunk, piece, target):
+        if not line:
+            return chunk * groups + me
+        if target is near:
+            return slot(chunk, 1, 0)
+        inner = lax.rem((me + 1) // 2, 2)
+        return slot(chunk, 2, 0) + inner * (1 + piece)
+
+    def slot_here(chunk, role, piece, source):
+        return slot(chunk, role, piece) if line else chunk * groups + source
+
+    def wide(chunk, piece, split, source, target, place=0, kinds=slice(None)):
         begin, size = cut(chunk, piece, split)
         return pltpu.make_async_remote_copy(
-            src_ref=sent.at[chunk, :, pl.ds(target * capacity + begin, size)],
-            dst_ref=got[chunk].at[:, pl.ds(source * capacity + begin, size)],
-            send_sem=wide_send.at[chunk],
-            recv_sem=wide_recv.at[chunk + piece, source],
+            src_ref=sent.at[chunk, kinds, pl.ds(target * capacity + begin, size)],
+            dst_ref=got[chunk].at[kinds, pl.ds(source * capacity + begin, size)],
+            send_sem=wide_send.at[0],
+            recv_sem=wide_recv.at[place],
             device_id={"tensor": target},
             device_id_type=MESH,
         )
 
-    def wide_sent(chunk):
-        everything = sent.at[chunk, :, pl.ds(0, (groups - 1) * capacity)]
-        return pltpu.make_async_remote_copy(
-            src_ref=everything,
-            dst_ref=everything,
-            send_sem=wide_send.at[chunk],
-            recv_sem=wide_recv.at[chunk, 0],
-            device_id={"tensor": targets[0]},
-            device_id_type=MESH,
+    def own_far_load(chunk, k):
+        return pltpu.make_async_copy(
+            grads.at[0, :, band(chunk, far(k)), :],
+            own_far.at[chunk, k - 1],
+            own_sem.at[1 + chunk * (chips - 1) + k - 1],
+        )
+
+    def own_here_load(chunk):
+        return pltpu.make_async_copy(
+            grads.at[0, :, band(chunk, mine), :], own_here[chunk], own_sem.at[0]
         )
 
     def grad_loads(chunk):
-        return [
-            pltpu.make_async_copy(
-                grads.at[0, :, band(chunk, far(k)), :], own_far.at[chunk, k - 1], own_sem.at[chunk, k]
-            )
-            if k
-            else pltpu.make_async_copy(
-                grads.at[0, :, band(chunk, mine), :], own_here[chunk], own_sem.at[chunk, 0]
-            )
-            for k in range(chips)
-        ]
+        return [own_far_load(chunk, k) for k in across] + [own_here_load(chunk)]
 
     def twin_copy(chunk, k):
         return pltpu.make_async_remote_copy(
             src_ref=grads.at[0, :, band(chunk, far_twin(k)), :],
             dst_ref=twin_far.at[chunk, k - 1] if k else twin_here[chunk],
             send_sem=twin_send.at[k],
-            recv_sem=twin_recv.at[chunk, k],
+            recv_sem=twin_recv.at[1 + chunk * (chips - 1) + k - 1 if k else 0],
             device_id={"dp": twin},
             device_id_type=MESH,
         )
@@ -225,8 +245,8 @@
         return pltpu.make_async_remote_copy(
             src_ref=own_far.at[chunk, k - 1],
             dst_ref=far_here[chunk][chips - k - 1],
-            send_sem=far_send.at[k],
-            recv_sem=far_recv.at[chunk, chips - k],
+            send_sem=far_send.at[k - 1],
+            recv_sem=far_recv.at[chunk, chips - k - 1],
             device_id={"dp": far(k)},
             device_id_type=MESH,
         )
@@ -235,8 +255,8 @@
         return pltpu.make_async_remote_copy(
             src_ref=own_far.at[chunk, chips - k - 1],
             dst_ref=far_here[chunk][k - 1],
-            send_sem=far_send.at[chips - k],
-            recv_sem=far_recv.at[chunk, k],
+            send_sem=far_send.at[chips - k - 1],
+            recv_sem=far_recv.at[chunk, k - 1],
             device_id={"dp": far(k)},
             device_id_type=MESH,
         )
@@ -245,13 +265,13 @@
         chunk, role, piece = entry
         if role is None:
             return 0, groups * capacity
-        begin, size = cut(chunk, piece, role > 1)
+        begin, size = cut(chunk, piece, role > 2)
         return sources[role] * capacity + begin, size
 
     def rows_of(entry):
         if entry[1] is None:
             return [(source, 0, capacity) for source in range(groups)]
-        return [(sources[entry[1]], *cut(entry[0], entry[2], entry[1] > 1))]
+        return [(sources[entry[1]], *cut(entry[0], entry[2], entry[1] > 2))]
 
     def spread(step, owner, target, send, recv):
         start, size = extent(order[step])
@@ -272,7 +292,10 @@
         return spread(step, mine, twin, last_send.at[0], twin_last.at[0])
 
     def relay(step, k):
-        return spread(step, far(k), twin, relay_send.at[k], relay_recv.at[k])
+        return spread(step, far(k), twin, relay_send.at[k - 1], relay_recv.at[k - 1])
+
+    def direct_spread(step, k):
+        return spread(step, mine, far_twin(k), direct_send.at[k - 1], relay_recv.at[chips - k - 1])
 
     def whole(owner, send, recv):
         here = weights.at[:, pl.ds(pl.multiple_of(owner * rows, ROWS), rows), :]
@@ -297,7 +320,6 @@
 
     fetch = pltpu.make_async_copy(dest, flat, table_sem.at[0])
     fetch.start()
-    start(loads(0))
     barrier = pltpu.get_barrier_semaphore()
     for target in targets:
         pl.semaphore_signal(barrier, inc=1, device_id={"tensor": target}, device_id_type=MESH)
@@ -306,22 +328,19 @@
         pl.semaphore_signal(barrier, inc=1, device_id={"dp": far(k)}, device_id_type=MESH)
     half = table_out.shape[0] // 2
     fetch.wait()
-    table_out[...] = routes(flat[...], groups, slots, me)[:, : table_out.shape[1]]
-    start(grad_loads(0))
+    start(loads(0))
+    table_out[...] = routes(flat[...], groups, slots, capacity, me)[:, : table_out.shape[1]]
     copy = pltpu.make_async_copy(table_out, table, table_sem.at[1])
     copy.start()
     copy.wait()
 
-    def pack(chunk, target, to_got=False):
+    def pack(chunk, target, to_got=False, kinds=range(3)):
         def one(i):
             s = jnp.maximum(table[half + target, i], 0)
             j = target * capacity + i
-            values = (
-                encode(raw[chunk % 2][0, s]),
-                raw[chunk % 2][1, s].astype(jnp.bfloat16),
-                raw[chunk % 2][2, s].astype(jnp.bfloat16),
-            )
-            for k, value in enumerate(values):
+            for k in kinds:
+                value = raw[chunk % 2][k][s]
+                value = encode(value) if k == 0 else value.astype(jnp.bfloat16)
                 if to_got:
                     got[chunk][k, j] = value
                 else:
@@ -336,26 +355,39 @@
         waiting[:] = copies
 
     for chunk in range(chunks):
-        loaded(chunk).wait()
-        if chunk == 0:
-            for other in range(1, chunks):
-                start(grad_loads(other))
-            if chunks > 1:
-                start(loads(1))
+        if chunk:
+            for load in loads(chunk):
+                load.wait()
         split = chunk == chunks - 1 and len(cuts) > 1
         for i, target in enumerate(targets):
+            if chunk == 0 and i == 0:
+                for k, load in enumerate(loads(0)):
+                    load.wait()
+                    pack(0, target, kinds=(k,))
+                    if k == 0:
+                        pl.semaphore_wait(barrier, groups - 1 + chips)
+                        start([twin_copy(0, i) for i in reversed(range(chips))])
+                    if not split:
+                        send([
+                            wide(0, 0, False, me, target, slot_there(0, 0, target), pl.ds(k, 1))
+                        ])
+                        if k == 0:
+                            send([])
+                for other in range(chunks):
+                    start(grad_loads(other))
+                if chunks > 1:
+                    start(loads(1))
+                for other in range(1, chunks):
+                    start([twin_copy(other, k) for k in reversed(range(chips))])
+                continue
             pack(chunk, target)
-            if chunk == 0 and i == 0:
-                pl.semaphore_wait(barrier, groups - 1 + chips)
-                for other in range(chunks):
-                    start([twin_copy(other, k) for k in reversed(range(chips))])
             if not split:
-                send([wide(chunk, 0, False, me, target)])
+                send([wide(chunk, 0, False, me, target, slot_there(chunk, 0, target))])
         if split:
             send(
-                [wide(chunk, 0, False, me, targets[-1])]
+                [wide(chunk, 0, False, me, targets[-1], slot_there(chunk, 0, targets[-1]))]
                 + [
-                    wide(chunk, i, True, me, target)
+                    wide(chunk, i, True, me, target, slot_there(chunk, i, target))
                     for i in range(len(cuts))
                     for target in targets[:-1]
                 ]
@@ -364,9 +396,8 @@
         if chunk + 2 < chunks:
             start(loads(chunk + 2))
         send([])
-        for copy in grad_loads(chunk):
-            copy.wait()
         for k in across:
+            own_far_load(chunk, k).wait()
             twin_copy(chunk, k).wait_recv()
 
             def join(s, chunk=chunk, k=k):
@@ -378,25 +409,30 @@
             loop(0, slots, join)
             far_copy(chunk, k).start()
 
+    def far_got(step, k):
+        return spread(step, far(k), twin, relay_send.at[k - 1], last_recv.at[step, k - 1])
+
     def pass_on(step):
         for k in across:
-            far_wait_here = spread(step, far(k), twin, relay_send.at[k], last_recv.at[step, k - 1])
-            far_wait_here.wait_recv()
+            far_got(step, k).wait_recv()
             relay(step, k).start()
 
+    pltpu.make_async_copy(own_far.at[:, 0], own_far.at[:, 0], own_sem.at[0]).wait()
+    every(twin_far.at[:, 0], twin_send.at[0], twin_recv.at[0]).wait_recv()
     ready = set()
+    behind = []
     for step, entry in enumerate(order):
         chunk, role, piece = entry
         if chunk not in ready:
             ready.add(chunk)
-            twin_copy(chunk, 0).wait_recv()
             for k in across:
                 far_wait(chunk, k).wait_recv()
         if role is None:
             for source in sources[1:]:
-                wide(chunk, 0, False, source, me).wait_recv()
+                wide(chunk, 0, False, source, me, slot_here(chunk, 0, 0, source)).wait_recv()
         elif role > 0:
-            wide(chunk, piece, role > 1, sources[role], me).wait_recv()
+            place = slot_here(chunk, role, piece, sources[role])
+            wide(chunk, piece, role > 2, sources[role], me, place).wait_recv()
 
         def update(source, i, chunk=chunk):
             p = jnp.maximum(table[source, i], 0)
@@ -418,23 +454,35 @@
         for source, begin, size in rows_of(entry):
             loop(begin, size, functools.partial(update, source))
         start([far_spread(step, k) for k in across])
+        if step >= relayed:
+            start([direct_spread(step, k) for k in across])
+        else:
+            behind.append(step)
         twin_spread(step).start()
-        if step >= LAG:
-            pass_on(step - LAG)
-    for step in range(max(len(order) - LAG, 0), len(order)):
+        while len(behind) > (LAG if chunk < chunks - 1 else 2) or (behind and step >= relayed):
+            pass_on(behind.pop(0))
+    for step in behind:
         pass_on(step)
+    for step in range(relayed, len(order)):
+        for k in across:
+            far_got(step, k).wait_recv()
 
     whole(twin, last_send.at[0], twin_last.at[0]).wait_recv()
+    for k in across:
+        whole(far_twin(k), relay_send.at[k - 1], relay_recv.at[k - 1]).wait_recv()
     whole(mine, last_send.at[0], twin_last.at[0]).wait_send()
     for k in across:
         whole(mine, last_send.at[k], twin_last.at[0]).wait_send()
-        whole(far(k), relay_send.at[k], relay_recv.at[k]).wait_send()
-        whole(far_twin(k), relay_send.at[k], relay_recv.at[k]).wait_recv()
-        every(own_far.at[:, k - 1], far_send.at[k], far_recv.at[0, 0]).wait_send()
+        passed = weights.at[pl.ds(0, groups * capacity - straight * ROWS // rows), pl.ds(0, rows)]
+        every(passed, relay_send.at[k - 1], twin_last.at[0]).wait_send()
+        if straight:
+            passed = weights.at[pl.ds(0, straight), pl.ds(0, ROWS)]
+            every(passed, direct_send.at[k - 1], twin_last.at[0]).wait_send()
+        every(own_far.at[:, k - 1], far_send.at[k - 1], twin_last.at[0]).wait_send()
     for k in range(chips):
-        every(twin_far.at[:, max(k - 1, 0)], twin_send.at[k], twin_recv.at[0, 0]).wait_send()
-    for chunk in range(chunks):
-        wide_sent(chunk).wait_send()
+        every(twin_far.at[:, max(k - 1, 0)], twin_send.at[k], twin_last.at[0]).wait_send()
+    gone = sent.at[:, :, pl.ds(0, (groups - 1) * capacity)]
+    every(gone, wide_send.at[0], twin_last.at[0]).wait_send()
 
 
 def place_kernel(
@@ -468,7 +516,7 @@
     chunks = rows // ROWS
     chips = replicas // 2
     length = groups * capacity
-    lines = 8 * pl.cdiv(groups, 8)
+    lines = lines_of(groups)
     wide = LANES * pl.cdiv(capacity, LANES)
     spare = -dest_table.shape[0] % LANES
     dest = jnp.pad(dest_table, (0, spare)) if spare else dest_table
@@ -499,7 +547,7 @@
         scratch_shapes=[
             pltpu.SMEM((2 * lines, wide), jnp.int32),
             pltpu.VMEM(dest.shape, jnp.int32),
-            [pltpu.VMEM((3, slots, ROWS, lanes), jnp.float32)] * 2,
+            [[pltpu.VMEM((slots, ROWS, lanes), jnp.float32)] * 3] * 2,
             pltpu.VMEM((chunks, 3, length, ROWS, lanes), half),
             [pltpu.VMEM((3, length, ROWS, lanes), half)] * chunks,
             [pltpu.VMEM((slots, ROWS, lanes), half)] * chunks,
@@ -508,19 +556,20 @@
             pltpu.VMEM((chunks, chips - 1, slots, ROWS, lanes), half),
             [[pltpu.VMEM((slots, ROWS, lanes), half)] * (chips - 1)] * chunks,
             dma((2,)),
-            dma((2,)),
-            dma((chunks, chips)),
-            dma((chunks,)),
-            dma((chunks + cuts - 1, groups)),
+            dma((2, 3)),
+            dma((1 + chunks * (chips - 1),)),
+            dma((1,)),
+            dma((3 * chunks + cuts - 1 if groups == LINE else chunks * groups,)),
             dma((chips,)),
-            dma((chunks, chips)),
-            dma((chips,)),
-            dma((chunks, chips)),
+            dma((1 + chunks * (chips - 1),)),
+            dma((chips - 1,)),
+            dma((chunks, chips - 1)),
             dma((chips,)),
             dma((steps, chips - 1)),
             dma((1,)),
-            dma((chips,)),
-            dma((chips,)),
+            dma((chips - 1,)),
+            dma((chips - 1,)),
+            dma((chips - 1,)),
         ],
         compiler_params=pltpu.CompilerParams(
             collective_id=0, has_side_effects=True, vmem_limit_bytes=scratch + SPARE

time: 174 us -> 172 us (0.989)
  Pallas kernels: 171 us -> 169 us
    pallas_call x1, Pallas kernels: 163 us -> 160 us  [exchange(): pl.pallas_call(functools.partial(exchange_kernel, groups, replicas, capac...]
where the time goes in v3:
time: 172 us; the launch traced here: 169 us
  Pallas kernels  169 us (98%)
    pallas_call x1, Pallas kernels, exchange(): pl.pallas_call(functools.partial(exchange_kernel, groups, replicas, capac...  160 us
    pallas_call x1, Pallas kernels, exchange(): pl.pallas_call(functools.partial(place_kernel, groups, capacity), out_sha...  8.2 us

profile of v3, /device:TPU:9, one launch (start us, length us, event | category | flops | bytes accessed | tf_op | source)
XLA Modules:
  0.0 169.3 jit_solution(13709186328808991227)
XLA Ops:
  0.6 160.5 %exchange.1 = (f32[288,32,128]{2,1,0:T(8,128)S(1)}, f32[288,32,128]{2,1,0:T(8,128)S(1)}, f32[288,32,128]{2,1,0:T(8,128)S(1)}, bf16[288,128,128]{2,1,0:T(8,128)(2,1)S(1)}, s32[8,128]{1,0:T(8,128)S(1)}) custom-call(s32[9,128]{1,0:T(8,128)} %bitcast.1, f32[288,32,128]{2,1,0:T(8,128)} %weight.1, f32[288,32,128]{2,1,0:T(8,128)} %first.1, f32[288,32,128]{2,1,0:T(8,128)} %second.1, ...), custom_call_target="tpu_custom_call" | custom-call | tf_op jit(solution)/shard_map/exchange/pallas_call | solution.py:538
  161.1 8.2 %place.1 = (f32[288,32,128]{2,1,0:T(8,128)}, f32[288,32,128]{2,1,0:T(8,128)}, f32[288,32,128]{2,1,0:T(8,128)}, bf16[288,128,128]{2,1,0:T(8,128)(2,1)}) custom-call(s32[8,128]{1,0:T(8,128)S(1)} %get-tuple-element.9.table, f32[288,32,128]{2,1,0:T(8,128)S(1)} %get-tuple-element.10.weight, f32[288,32,128]{2,1,0:T(8,128)S(1)} %get-tuple-element.11.first, ...), custom_call_target="tpu_custom_call" | custom-call | tf_op jit(solution)/shard_map/place/pallas_call | solution.py:580

commit v4 on v3

--- a/solution.py
+++ b/solution.py
@@ -37,6 +37,7 @@
 LINE = 4
 LAG = 4
 DIRECT = 2
+SHARES = 4
 MESH = pl.DeviceIdType.MESH
 
 
@@ -136,8 +137,8 @@
 def exchange_kernel(
     groups, replicas, capacity, chunks,
     dest, weight, first, second, grads,
-    weight_new, first_new, second_new, weights, table_out,
-    table, flat,
+    weight_new, first_new, second_new, weights, table,
+    table_out, flat,
     raw, sent, got, own_here, own_far, twin_here, twin_far, far_here,
     table_sem, load_sem, own_sem, wide_send, wide_recv, twin_send, twin_recv, far_send, far_recv,
     last_send, last_recv, twin_last, relay_send, relay_recv, direct_send,
@@ -158,7 +159,10 @@
     if line:
         side = me // 2
         near = me + 1 - 2 * lax.rem(me, 2)
-        targets = [3 - me, lax.rem(me + 2, 4), near]
+        inner = lax.rem((me + 1) // 2, 2)
+        opposite, facing = lax.rem(me + 2, 4), 3 - me
+        first_target = inner * opposite + (1 - inner) * facing
+        targets = [first_target, opposite + facing - first_target, near]
         sources = [me, near, 3 - 3 * side, 2 - side]
     else:
         targets = [lax.rem(me + k, groups) for k in range(1, groups)]
@@ -175,15 +179,20 @@
             return pl.ds(chunk * ROWS, ROWS)
         return pl.ds(pl.multiple_of(owner * rows + chunk * ROWS, ROWS), ROWS)
 
-    def loads(chunk):
+    def loads(chunk, kinds=range(3)):
+        share = slots // SHARES if chunk == 0 and slots % SHARES == 0 else slots
         return [
             pltpu.make_async_copy(
-                ref.at[:, band(chunk), :],
-                raw[chunk % 2][k],
+                (weight, first, second)[k].at[pl.ds(begin, share), band(chunk), :],
+                raw[chunk % 2][k].at[pl.ds(begin, share)],
                 load_sem.at[chunk % 2, k],
             )
-            for k, ref in enumerate((weight, first, second))
+            for k in kinds
+            for begin in range(0, slots, share)
         ]
+
+    def loaded(chunk, k):
+        pltpu.make_async_copy(raw[chunk % 2][k], raw[chunk % 2][k], load_sem.at[chunk % 2, k]).wait()
 
     def cut(chunk, piece, split):
         if chunk == chunks - 1 and split:
@@ -199,7 +208,6 @@
             return chunk * groups + me
         if target is near:
             return slot(chunk, 1, 0)
-        inner = lax.rem((me + 1) // 2, 2)
         return slot(chunk, 2, 0) + inner * (1 + piece)
 
     def slot_here(chunk, role, piece, source):
@@ -327,12 +335,14 @@
     for k in across:
         pl.semaphore_signal(barrier, inc=1, device_id={"dp": far(k)}, device_id_type=MESH)
     half = table_out.shape[0] // 2
+    start(loads(0, [0]))
     fetch.wait()
-    start(loads(0))
     table_out[...] = routes(flat[...], groups, slots, capacity, me)[:, : table_out.shape[1]]
     copy = pltpu.make_async_copy(table_out, table, table_sem.at[1])
     copy.start()
     copy.wait()
+    loaded(0, 0)
+    start(loads(0, [1, 2]))
 
     def pack(chunk, target, to_got=False, kinds=range(3)):
         def one(i):
@@ -356,13 +366,14 @@
 
     for chunk in range(chunks):
         if chunk:
-            for load in loads(chunk):
-                load.wait()
+            for k in range(3):
+                loaded(chunk, k)
         split = chunk == chunks - 1 and len(cuts) > 1
         for i, target in enumerate(targets):
             if chunk == 0 and i == 0:
-                for k, load in enumerate(loads(0)):
-                    load.wait()
+                for k in range(3):
+                    if k:
+                        loaded(0, k)
                     pack(0, target, kinds=(k,))
                     if k == 0:
                         pl.semaphore_wait(barrier, groups - 1 + chips)
@@ -540,12 +551,12 @@
         out_shape=(
             whole, whole, whole,
             pltpu.VMEM((length,) + grads.shape[2:], half),
-            pltpu.VMEM((2 * lines, wide), jnp.int32),
+            pltpu.SMEM((2 * lines, wide), jnp.int32),
         ),
         in_specs=[anywhere] * 5,
-        out_specs=(near,) * 5,
+        out_specs=(near,) * 4 + (table,),
         scratch_shapes=[
-            pltpu.SMEM((2 * lines, wide), jnp.int32),
+            pltpu.VMEM((2 * lines, wide), jnp.int32),
             pltpu.VMEM(dest.shape, jnp.int32),
             [[pltpu.VMEM((slots, ROWS, lanes), jnp.float32)] * 3] * 2,
             pltpu.VMEM((chunks, 3, length, ROWS, lanes), half),

time: 172 us -> 171 us (level)
  no operation moved by 1% of the time
where the time goes in v4:
time: 171 us; the launch traced here: 169 us
  Pallas kernels  168 us (98%)
    pallas_call x1, Pallas kernels, exchange(): pl.pallas_call(functools.partial(exchange_kernel, groups, replicas, capac...  161 us
    pallas_call x1, Pallas kernels, exchange(): pl.pallas_call(functools.partial(place_kernel, groups, capacity), out_sha...  7.6 us

profile of v4, /device:TPU:9, one launch (start us, length us, event | category | flops | bytes accessed | tf_op | source)
XLA Modules:
  0.0 168.8 jit_solution(1539272646854716891)
XLA Ops:
  0.6 160.5 %exchange.1 = (f32[288,32,128]{2,1,0:T(8,128)S(1)}, f32[288,32,128]{2,1,0:T(8,128)S(1)}, f32[288,32,128]{2,1,0:T(8,128)S(1)}, bf16[288,128,128]{2,1,0:T(8,128)(2,1)S(1)}, s32[8,128]{1,0:T(8,128)S(4)}) custom-call(s32[9,128]{1,0:T(8,128)} %bitcast.1, f32[288,32,128]{2,1,0:T(8,128)} %weight.1, f32[288,32,128]{2,1,0:T(8,128)} %first.1, f32[288,32,128]{2,1,0:T(8,128)} %second.1, ...), custom_call_target="tpu_custom_call" | custom-call | tf_op jit(solution)/shard_map/exchange/pallas_call | solution.py:549
  161.2 7.6 %place.1 = (f32[288,32,128]{2,1,0:T(8,128)}, f32[288,32,128]{2,1,0:T(8,128)}, f32[288,32,128]{2,1,0:T(8,128)}, bf16[288,128,128]{2,1,0:T(8,128)(2,1)}) custom-call(s32[8,128]{1,0:T(8,128)S(4)} %get-tuple-element.9.table, f32[288,32,128]{2,1,0:T(8,128)S(1)} %get-tuple-element.10.weight, f32[288,32,128]{2,1,0:T(8,128)S(1)} %get-tuple-element.11.first, ...), custom_call_target="tpu_custom_call" | custom-call | tf_op jit(solution)/shard_map/place/pallas_call | solution.py:591

commit v5 on v4

--- a/solution.py
+++ b/solution.py
@@ -38,6 +38,7 @@
 LAG = 4
 DIRECT = 2
 SHARES = 4
+EARLY = 16
 MESH = pl.DeviceIdType.MESH
 
 
@@ -213,8 +214,8 @@
     def slot_here(chunk, role, piece, source):
         return slot(chunk, role, piece) if line else chunk * groups + source
 
-    def wide(chunk, piece, split, source, target, place=0, kinds=slice(None)):
-        begin, size = cut(chunk, piece, split)
+    def wide(chunk, piece, split, source, target, place=0, kinds=slice(None), extent=None):
+        begin, size = extent or cut(chunk, piece, split)
         return pltpu.make_async_remote_copy(
             src_ref=sent.at[chunk, kinds, pl.ds(target * capacity + begin, size)],
             dst_ref=got[chunk].at[kinds, pl.ds(source * capacity + begin, size)],
@@ -344,7 +345,7 @@
     loaded(0, 0)
     start(loads(0, [1, 2]))
 
-    def pack(chunk, target, to_got=False, kinds=range(3)):
+    def pack(chunk, target, to_got=False, kinds=range(3), extent=(0, capacity)):
         def one(i):
             s = jnp.maximum(table[half + target, i], 0)
             j = target * capacity + i
@@ -356,7 +357,7 @@
                 else:
                     sent[chunk, k, j] = value
 
-        loop(0, capacity, one)
+        loop(*extent, one)
 
     waiting = []
 
@@ -374,16 +375,21 @@
                 for k in range(3):
                     if k:
                         loaded(0, k)
-                    pack(0, target, kinds=(k,))
+                    early = EARLY if k == 0 and capacity > EARLY and not split else capacity
+                    pack(0, target, kinds=(k,), extent=(0, early))
                     if k == 0:
                         pl.semaphore_wait(barrier, groups - 1 + chips)
                         start([twin_copy(0, i) for i in reversed(range(chips))])
                     if not split:
-                        send([
-                            wide(0, 0, False, me, target, slot_there(0, 0, target), pl.ds(k, 1))
-                        ])
+                        there = slot_there(0, 0, target)
+                        reach = (0, early)
+                        send([wide(0, 0, False, me, target, there, pl.ds(k, 1), reach)])
                         if k == 0:
                             send([])
+                        if early < capacity:
+                            reach = (early, capacity - early)
+                            pack(0, target, kinds=(k,), extent=reach)
+                            send([wide(0, 0, False, me, target, there, pl.ds(k, 1), reach)])
                 for other in range(chunks):
                     start(grad_loads(other))
                 if chunks > 1:
@@ -470,7 +476,7 @@
         else:
             behind.append(step)
         twin_spread(step).start()
-        while len(behind) > (LAG if chunk < chunks - 1 else 2) or (behind and step >= relayed):
+        while len(behind) > (LAG if chunk < chunks - 1 else 1 if step >= relayed else 2):
             pass_on(behind.pop(0))
     for step in behind:
         pass_on(step)

time: 171 us -> 171 us (level)
  no operation moved by 1% of the time
where the time goes in v5:
time: 171 us; the launch traced here: 169 us
  Pallas kernels  168 us (98%)
    pallas_call x1, Pallas kernels, exchange(): pl.pallas_call(functools.partial(exchange_kernel, groups, replicas, capac...  161 us
    pallas_call x1, Pallas kernels, exchange(): pl.pallas_call(functools.partial(place_kernel, groups, capacity), out_sha...  7.6 us

profile of v5, /device:TPU:9, one launch (start us, length us, event | category | flops | bytes accessed | tf_op | source)
XLA Modules:
  0.0 169.1 jit_solution(2995985501940808360)
XLA Ops:
  0.6 160.8 %exchange.1 = (f32[288,32,128]{2,1,0:T(8,128)S(1)}, f32[288,32,128]{2,1,0:T(8,128)S(1)}, f32[288,32,128]{2,1,0:T(8,128)S(1)}, bf16[288,128,128]{2,1,0:T(8,128)(2,1)S(1)}, s32[8,128]{1,0:T(8,128)S(4)}) custom-call(s32[9,128]{1,0:T(8,128)} %bitcast.1, f32[288,32,128]{2,1,0:T(8,128)} %weight.1, f32[288,32,128]{2,1,0:T(8,128)} %first.1, f32[288,32,128]{2,1,0:T(8,128)} %second.1, ...), custom_call_target="tpu_custom_call" | custom-call | tf_op jit(solution)/shard_map/exchange/pallas_call | solution.py:555
  161.5 7.6 %place.1 = (f32[288,32,128]{2,1,0:T(8,128)}, f32[288,32,128]{2,1,0:T(8,128)}, f32[288,32,128]{2,1,0:T(8,128)}, bf16[288,128,128]{2,1,0:T(8,128)(2,1)}) custom-call(s32[8,128]{1,0:T(8,128)S(4)} %get-tuple-element.9.table, f32[288,32,128]{2,1,0:T(8,128)S(1)} %get-tuple-element.10.weight, f32[288,32,128]{2,1,0:T(8,128)S(1)} %get-tuple-element.11.first, ...), custom_call_target="tpu_custom_call" | custom-call | tf_op jit(solution)/shard_map/place/pallas_call | solution.py:597
